TPU v7x, 32 devices: a whole 2x2x4 slice. The times are simulated.
32 devices in a mesh: blk: 8 (over y, x, core), member: 4 (over z).
Axes of the slice: x: 2, y: 2, z: 4, core: 2. Of those that a mesh axis runs over, the one named last changes fastest.
Arguments:
- coords: float32 [2048, 64], P(('blk', 'member')), may hold values from -6 to 6
- codes: int32 [2048, 4, 512], P('blk', 'member'), may hold values from 0 to 255
- classes: int32 [2048, 4, 512], P('blk', 'member'), may hold values from 0 to 3
Outputs:
- final_coords: float32 [2048, 64], P(('blk', 'member'))
All inputs are finite; a program needn't handle non-finite values.
Results may differ from a plain program's by a relative error of at most 0.0003.
Values sent between devices are 32-bit elements; how exact they have to be, the bound alone decides.
A program may use at most 64 MiB of HBM per device.

v0:
```python
import jax
import jax.numpy as jnp
from jax import lax
from jax.sharding import PartitionSpec as P

ITERS = 3


code_step = 0.1
epsilon = 1e-06


def body(coords, codes, classes):
    rows_dev = coords.shape[0]
    n_blocks = lax.axis_size("blk")
    n_members = lax.axis_size("member")
    band_len = rows_dev * n_members
    slab = rows_dev * n_blocks
    blk_index = lax.axis_index("blk")
    mem_index = lax.axis_index("member")
    code_tile = codes.reshape(band_len, slab)
    class_tile = classes.reshape(band_len, slab)
    row_ids = blk_index * band_len + lax.broadcasted_iota(jnp.int32, (band_len, slab), 0)
    col_pos = lax.broadcasted_iota(jnp.int32, (band_len, slab), 1)
    col_ids = col_pos // rows_dev * band_len + mem_index * rows_dev + col_pos % rows_dev
    self_pair = row_ids == col_ids
    weights = jnp.where(self_pair, jnp.float32(0.0), 1.0 / (1.0 + class_tile.astype(jnp.float32)))
    targeted = weights * (code_tile.astype(jnp.float32) + 1.0) * code_step
    weight_rows = jnp.sum(weights, axis=1)
    own_rows = coords
    band = coords
    for step in range(ITERS):
        band = lax.all_gather(own_rows, "member", axis=0, tiled=True)
        columns = lax.all_gather(own_rows, "blk", axis=0, tiled=True)
        gram = jnp.dot(band, columns.T, precision=lax.Precision.HIGHEST)
        dist_sq = (
            jnp.sum(band * band, axis=1)[:, None]
            + jnp.sum(columns * columns, axis=1)[None, :]
            - 2.0 * gram
        )
        dist_sq = jnp.where(self_pair, jnp.float32(1.0), dist_sq)
        ratio = targeted / jnp.sqrt(dist_sq + epsilon)
        numer = jnp.dot(weights - ratio, columns, precision=lax.Precision.HIGHEST)
        numer, ratio_rows = (numer, jnp.sum(ratio, axis=1))
        numer, ratio_rows, weight_own = (
            lax.psum_scatter(numer, "member", scatter_dimension=0, tiled=True),
            lax.psum_scatter(ratio_rows, "member", scatter_dimension=0, tiled=True),
            lax.psum_scatter(weight_rows, "member", scatter_dimension=0, tiled=True),
        )
        own_rows = (numer + own_rows * ratio_rows[:, None]) / weight_own[:, None]
    return own_rows


def solution(mesh):
    in_specs = (P(("blk", "member"), None), P("blk", "member", None), P("blk", "member", None))
    out_specs = P(("blk", "member"), None)
    return jax.shard_map(body, mesh=mesh, in_specs=in_specs, out_specs=out_specs, check_vma=False)
```

profile of v0, /device:TPU:0, one launch (start us, length us, event | category | flops | bytes accessed | tf_op | source)
XLA Modules:
  0.0 148.6 jit_solution(12957165185318063440)
XLA Ops:
  6.5 0.0 copy-start
  6.5 0.0 reduce-scatter.4.cloned.1.call-start
  6.6 15.4 %all_gather.18 = f32[256,64]{1,0:T(8,128)S(1)} all-gather(f32[64,64]{1,0:T(8,128)} %param.3), channel_id=1, replica_groups=mesh['blk'=8,'member'=4] {'member'}, dimensions={0}, use_global_device_ids=true | all-gather | bytes 81920 | tf_op jit(solution)/shard_map/all_gather | solution.py:33
  22.0 9.5 %all_gather.19 = f32[512,64]{1,0:T(8,128)S(1)} all-gather(f32[64,64]{1,0:T(8,128)} %param.3), channel_id=1, replica_groups=mesh['blk'=8,'member'=4] {'blk'}, dimensions={0}, use_global_device_ids=true | all-gather | bytes 147456 | tf_op jit(solution)/shard_map/all_gather | solution.py:34
  31.5 0.1 multiply_reduce_fusion.5
  31.6 0.1 multiply_reduce_fusion.2
  31.8 0.0 copy-done
  31.8 1.9 %fusion.32 = (f32[256]{0:T(256)S(1)}, f32[256,512]{1,0:T(8,128)S(1)}) fusion(f32[256,64]{1,0:T(8,128)S(1)} %all_gather.18, f32[512,64]{1,0:T(8,128)S(1)} %all_gather.19, f32[512]{0:T(512)S(1)} %multiply_reduce_fusion.2, f32[256]{0:T(256)S(1)} %multiply_reduce_fusion.5, s32[256,1,512]{2,1,0:T(1,128)} %param.4, s32[256,1,512]{2,1,0:T(1,128)S(1)} %copy-done, ...), kind=kOutput, calls=%fused_computation.54 | convolution fusion | flops 103415552 | bytes 1783812 | tf_op jit(solution)/shard_map/dot_general | solution.py:35
  33.7 1.3 fusion.23
  35.0 0.0 reduce-scatter.4.cloned.1.call-update
  35.0 0.0 reduce-scatter.6.cloned.1.call-start
  35.1 0.0 copy-start.3
  35.1 0.6 copy-done.3
  35.7 0.6 dynamic-slice
  37.0 0.0 copy-start.1
  37.0 0.2 fusion.31
  37.2 0.0 copy-start.2
  37.2 12.2 %all-reduce.4 = (f32[256]{0:T(256)S(1)}, f32[256]{0:T(256)S(1)}) all-reduce(f32[256]{0:T(256)S(1)} %fusion.31, f32[256]{0:T(256)S(1)} %get-tuple-element.7), channel_id=4, replica_groups=mesh['blk'=8,'member'=4] {'member'}, use_global_device_ids=true, to_apply=%region_6.7.clone | all-reduce | flops 512 | bytes 4096
  49.4 0.1 dynamic-slice.3
  49.5 0.1 dynamic-slice.1
  49.6 5.4 %reduce-scatter.4.cloned.1.call-done = f32[64,64]{1,0:T(8,128)} async-done(((f32[256,64]{1,0:T(8,128)}), f32[64,64]{1,0:T(8,128)}) %reduce-scatter.4.cloned.1.call-update) | async-done | bytes 16400 | tf_op jit(solution)/shard_map/reduce_scatter | solution.py:46
  55.0 0.0 copy-done.1
  55.0 0.8 add_divide_fusion.2
  55.8 13.3 %all_gather.20 = f32[256,64]{1,0:T(8,128)S(1)} all-gather(f32[64,64]{1,0:T(8,128)S(1)} %add_divide_fusion.2), channel_id=1, replica_groups=mesh['blk'=8,'member'=4] {'member'}, dimensions={0}, use_global_device_ids=true | all-gather | bytes 81920 | tf_op jit(solution)/shard_map/all_gather | solution.py:33
  69.2 9.4 %all_gather.21 = f32[512,64]{1,0:T(8,128)S(1)} all-gather(f32[64,64]{1,0:T(8,128)S(1)} %add_divide_fusion.2), channel_id=1, replica_groups=mesh['blk'=8,'member'=4] {'blk'}, dimensions={0}, use_global_device_ids=true | all-gather | bytes 147456 | tf_op jit(solution)/shard_map/all_gather | solution.py:34
  78.5 0.1 multiply_reduce_fusion.4
  78.7 0.1 multiply_reduce_fusion.1
  78.8 0.0 copy-done.2
  78.8 0.9 fusion.33
  79.7 1.3 fusion.21
  81.0 0.0 reduce-scatter.6.cloned.1.call-update
  81.0 0.0 reduce-scatter.8.cloned.1.call-start
  81.1 9.0 %all-reduce.2 = f32[256]{0:T(256)S(1)} all-reduce(f32[256]{0:T(256)S(1)} %get-tuple-element.9), channel_id=6, replica_groups=mesh['blk'=8,'member'=4] {'member'}, use_global_device_ids=true, to_apply=%region_11.12.clone | all-reduce | flops 256 | bytes 2048
  90.0 0.1 dynamic-slice.5
  90.1 7.7 %reduce-scatter.6.cloned.1.call-done = f32[64,64]{1,0:T(8,128)} async-done(((f32[256,64]{1,0:T(8,128)}), f32[64,64]{1,0:T(8,128)}) %reduce-scatter.6.cloned.1.call-update) | async-done | bytes 16400 | tf_op jit(solution)/shard_map/reduce_scatter | solution.py:46
  97.9 0.8 add_divide_fusion.1
  98.7 13.4 %all_gather.22 = f32[256,64]{1,0:T(8,128)S(1)} all-gather(f32[64,64]{1,0:T(8,128)S(1)} %add_divide_fusion.1), channel_id=1, replica_groups=mesh['blk'=8,'member'=4] {'member'}, dimensions={0}, use_global_device_ids=true | all-gather | bytes 81920 | tf_op jit(solution)/shard_map/all_gather | solution.py:33
  112.1 9.3 %all_gather.23 = f32[512,64]{1,0:T(8,128)S(1)} all-gather(f32[64,64]{1,0:T(8,128)S(1)} %add_divide_fusion.1), channel_id=1, replica_groups=mesh['blk'=8,'member'=4] {'blk'}, dimensions={0}, use_global_device_ids=true | all-gather | bytes 147456 | tf_op jit(solution)/shard_map/all_gather | solution.py:34
  121.4 0.1 multiply_reduce_fusion.3
  121.5 0.1 multiply_reduce_fusion
  121.6 0.9 fusion.34
  122.5 1.3 fusion.19
  123.8 0.0 reduce-scatter.8.cloned.1.call-update
  123.9 8.9 %all-reduce.3 = f32[256]{0:T(256)S(1)} all-reduce(f32[256]{0:T(256)S(1)} %get-tuple-element.11), channel_id=8, replica_groups=mesh['blk'=8,'member'=4] {'member'}, use_global_device_ids=true, to_apply=%region_16.17.clone | all-reduce | flops 256 | bytes 2048
  132.8 0.1 dynamic-slice.7
  132.9 7.8 %reduce-scatter.8.cloned.1.call-done = f32[64,64]{1,0:T(8,128)} async-done(((f32[256,64]{1,0:T(8,128)}), f32[64,64]{1,0:T(8,128)}) %reduce-scatter.8.cloned.1.call-update) | async-done | bytes 16400 | tf_op jit(solution)/shard_map/reduce_scatter | solution.py:46
  140.7 1.5 add_divide_fusion
  (4 shorter events, 0.0 us)
Async XLA Ops:
  6.5 25.2 %copy-start = (s32[256,1,512]{2,1,0:T(1,128)S(1)}, s32[256,1,512]{2,1,0:T(1,128)}, u32[]{:S(2)}) copy-start(s32[256,1,512]{2,1,0:T(1,128)} %param.5) | copy-start | bytes 1572868
  6.5 48.5 %reduce-scatter.4.cloned.1.call-start = ((), (), s32[]{:S(2)}) async-start(), calls=%async_computation.3 | async-start | bytes 163840 | tf_op jit(solution)/shard_map/reduce_scatter | solution.py:46
  35.0 62.8 %reduce-scatter.6.cloned.1.call-start = ((), (), s32[]{:S(2)}) async-start(), calls=%async_computation.4 | async-start | bytes 163840 | tf_op jit(solution)/shard_map/reduce_scatter | solution.py:46
  35.1 0.7 copy-start.3
  37.0 18.0 %copy-start.1 = (f32[64,64]{1,0:T(8,128)S(1)}, f32[64,64]{1,0:T(8,128)}, u32[]{:S(2)}) copy-start(f32[64,64]{1,0:T(8,128)} %param.3) | copy-start | bytes 49156
  37.2 41.6 %copy-start.2 = (s32[256,1,512]{2,1,0:T(1,128)S(1)}, s32[256,1,512]{2,1,0:T(1,128)}, u32[]{:S(2)}) copy-start(s32[256,1,512]{2,1,0:T(1,128)} %param.4) | copy-start | bytes 1572868
  81.0 59.6 %reduce-scatter.8.cloned.1.call-start = ((), (), s32[]{:S(2)}) async-start(), calls=%async_computation.5 | async-start | bytes 163840 | tf_op jit(solution)/shard_map/reduce_scatter | solution.py:46
Sparse Core Ops, SparseCore 0:
  35.1 19.7 reduce-scatter.3
  81.1 16.6 reduce-scatter.5
  124.0 16.6 reduce-scatter.7
where the time goes:
time: 149 us
  blocking collectives  100 us (67%)
  waiting for transfers between devices  21 us (14%)
  between operations  13.9 us (9%)
  matrix products  7.56 us (5%)
  other arithmetic  4.12 us (3%)
  local copies, waits for them, and re-layouts  1.55 us (1%)
    all_gather x3, blocking collectives, body(): band = lax.all_gather(own_rows, 'member', axis=0, tiled=True)  42.2 us
    unnamed x3, blocking collectives  30.1 us
    all_gather x3, blocking collectives, body(): columns = lax.all_gather(own_rows, 'blk', axis=0, tiled=True)  28.1 us
    reduce_scatter x3, waiting for transfers between devices, body(): lax.psum_scatter(numer, 'member', scatter_dimension=0, tiled=True)  21 us
    dot_general x3, matrix products, body(): numer = jnp.dot(weights - ratio, columns, precision=lax.Precision.HIGHEST)  3.9 us
    dot_general x3, matrix products, body(): gram = jnp.dot(band, columns.T, precision=lax.Precision.HIGHEST)  3.67 us
    div x3, other arithmetic, body(): own_rows = (numer + own_rows * ratio_rows[:, None]) / weight_own[:, None]  3.13 us
  transfers between devices with their start and end apart: 3, of which 3 were waited for; matrix products, arithmetic and copies ran while one was open for 1% of the time, Pallas kernels for 0%

commit v1 on v0

v1 whole, which is shorter than its diff:
```python
import functools

import jax
import jax.numpy as jnp
from jax import lax
from jax.experimental import pallas as pl
from jax.experimental.pallas import tpu as pltpu
from jax.sharding import PartitionSpec as P

ITERS = 3
code_step = 0.1
epsilon = 1e-06

F32 = jnp.float32
BF16 = jnp.bfloat16
LANES = 128


def split3(x):
    high = x.astype(BF16).astype(F32)
    rest = x - high
    mid = rest.astype(BF16).astype(F32)
    return high, mid, rest - mid


def doubled(packed):
    n, half, width = packed.shape
    low = lax.broadcasted_iota(jnp.int32, packed.shape, 2) < width // 2
    swapped = jnp.concatenate([packed[..., width // 2:], packed[..., : width // 2]], axis=2)
    return jnp.concatenate([jnp.where(low, packed, swapped), jnp.where(low, swapped, packed)], axis=1).reshape(n * 2 * half, width)


def pack(twice):
    half, width = twice.shape[0] // 2, twice.shape[1]
    low = lax.broadcasted_iota(jnp.int32, (half, width), 1) < width // 2
    return jnp.where(low, twice[:half], twice[half:])


def factors(twice):
    low = lax.broadcasted_iota(jnp.int32, twice.shape, 1) < twice.shape[1] // 2
    norm = 0.5 * jnp.sum(twice * twice, axis=1, keepdims=True)
    return low, split3(twice), split3(norm)


def norm_lanes(norm, rows, first, second):
    lane = lax.broadcasted_iota(jnp.int32, (rows, LANES), 1)
    ones = jnp.where((lane >= second) & (lane < second + 3), 1.0, 0.0)
    n0, n1, n2 = norm
    return jnp.where(lane == first, n0, jnp.where(lane == first + 1, n1, jnp.where(lane == first + 2, n2, ones))).astype(BF16)


def row_side(twice):
    low, (h, m, l), norm = factors(twice)
    parts = [(-2.0 * h).astype(BF16), (-2.0 * m).astype(BF16), (-2.0 * jnp.where(low, h, l)).astype(BF16)]
    return jnp.concatenate(parts + [norm_lanes(norm, twice.shape[0], 3, 0)], axis=1)


def column_side(twice):
    low, (h, m, l), norm = factors(twice)
    hm = jnp.where(low, h, m).astype(BF16)
    gram = jnp.concatenate([hm, hm, jnp.where(low, l, h).astype(BF16), norm_lanes(norm, twice.shape[0], 0, 3)], axis=1)
    return gram, jnp.concatenate([hm, jnp.where(low, l, 0.0).astype(BF16)], axis=1)


def kernel(n_blk, n_mem, coords, codes, classes, out,
           own, columns, band, weights, targets, code_tile, class_tile, part, part_in, wsum, wsum_in,
           load_sem, col_send, col_recv, band_send, band_recv, part_send, part_recv, w_send, w_recv):
    blk, mem = lax.axis_index("blk"), lax.axis_index("member")
    rows, width = coords.shape
    half = rows // 2
    slab = codes.shape[1]
    blks = [lax.rem(blk + k, n_blk) for k in range(1, n_blk)]
    mems = [lax.rem(mem + k, n_mem) for k in range(1, n_mem)]

    loads = [pltpu.make_async_copy(coords, out, load_sem.at[0]),
             pltpu.make_async_copy(codes, code_tile, load_sem.at[1]),
             pltpu.make_async_copy(classes, class_tile, load_sem.at[2])]
    for load in loads:
        load.start()
    barrier = pltpu.get_barrier_semaphore()
    for b in blks:
        pl.semaphore_signal(barrier, inc=1, device_id={"blk": b, "member": mem}, device_id_type=pl.DeviceIdType.MESH)
    for m in mems:
        pl.semaphore_signal(barrier, inc=1, device_id={"blk": blk, "member": m}, device_id_type=pl.DeviceIdType.MESH)

    def send(src, dst, ssem, rsem, b, m):
        return pltpu.make_async_remote_copy(src_ref=src, dst_ref=dst, send_sem=ssem, recv_sem=rsem,
                                            device_id={"blk": b, "member": m}, device_id_type=pl.DeviceIdType.MESH)

    def col_copy(it, b, slot):
        return send(own.at[it], columns.at[it, slot], col_send.at[it, b], col_recv.at[it, slot], b, mem)

    def band_copy(it, m, slot):
        return send(own.at[it], band.at[it, slot], band_send.at[it, m], band_recv.at[it, slot], blk, m)

    def part_copy(it, m, slot):
        return send(part.at[it, m], part_in.at[it, slot], part_send.at[it, m], part_recv.at[it, slot], blk, m)

    def w_copy(m, slot):
        return send(wsum.at[m], wsum_in.at[slot], w_send.at[m], w_recv.at[slot], blk, m)

    def spread(it, packed):
        own[it] = packed
        for b in blks:
            col_copy(it, b, blk).start()
        for m in mems:
            band_copy(it, m, mem).start()
        columns[it, blk] = packed
        band[it, mem] = packed

    loads[0].wait()
    start = out[...]
    first = jnp.concatenate([start[:half], start[half:]], axis=1)
    pl.semaphore_wait(barrier, n_blk + n_mem - 2)
    spread(0, first)

    loads[1].wait()
    loads[2].wait()
    order = mems + [mem]
    for m in order:
        at = pl.ds(pl.multiple_of(m * rows, rows), rows)
        row = lax.broadcasted_iota(jnp.int32, (rows, slab), 0)
        col = lax.broadcasted_iota(jnp.int32, (rows, slab), 1)
        self_at = jnp.where(m == mem, blk * rows, -slab - rows)
        weight = jnp.where(col == row + self_at, 0.0, 1.0 / (1.0 + class_tile[at, :].astype(F32)))
        weights[at, :] = weight
        targets[at, :] = weight * (code_tile[at, :].astype(F32) + 1.0) * code_step
        total = jnp.broadcast_to(jnp.sum(weight, axis=1, keepdims=True), (rows, 2 * width))
        wsum[m] = pack(total)
    for m in mems:
        w_copy(m, mem).start()

    for it in range(ITERS):
        for b in blks:
            col_copy(it, b, b).wait_recv()
        gram_side, sum_side = column_side(doubled(columns[it]))
        for m in mems:
            band_copy(it, m, m).wait_recv()
        total = None
        for m in order:
            at = pl.ds(pl.multiple_of(m * rows, rows), rows)
            twice = doubled(band[it, pl.ds(m, 1)])
            dist_sq = lax.dot_general(row_side(twice), gram_side, (((1,), (1,)), ((), ())), preferred_element_type=F32)
            ratio = targets[at, :] * lax.rsqrt(jnp.maximum(dist_sq, 0.0) + epsilon)
            pull = weights[at, :] - ratio
            high = pull.astype(BF16)
            low = (pull - high.astype(F32)).astype(BF16)
            sums = jnp.dot(jnp.concatenate([high, low], axis=0), sum_side, preferred_element_type=F32)
            sums = sums[:rows] + sums[rows:]
            sums = sums[:, : 2 * width] + sums[:, 2 * width:]
            sums = sums + jnp.concatenate([sums[:, width:], sums[:, :width]], axis=1)
            total = pack(sums + twice * jnp.sum(ratio, axis=1, keepdims=True))
            if m is not mem:
                part[it, m] = total
                part_copy(it, m, mem).start()
        if it == 0:
            weight_own = wsum[mem]
            for m in mems:
                w_copy(m, m).wait_recv()
                weight_own = weight_own + wsum_in[m]
        for m in mems:
            part_copy(it, m, m).wait_recv()
            total = total + part_in[it, m]
        total = total / weight_own
        if it < ITERS - 1:
            spread(it + 1, total)
    out[...] = jnp.concatenate([total[:, :width], total[:, width:]], axis=0)

    for m in mems:
        w_copy(m, m).wait_send()
    for it in range(ITERS):
        for b in blks:
            col_copy(it, b, b).wait_send()
        for m in mems:
            band_copy(it, m, m).wait_send()
            part_copy(it, m, m).wait_send()


def body(n_blk, n_mem, coords, codes, classes):
    rows, width = coords.shape
    band_len, slab = rows * n_mem, rows * n_blk
    packed = (rows // 2, 2 * width)
    dma = pltpu.SemaphoreType.DMA
    return pl.pallas_call(
        functools.partial(kernel, n_blk, n_mem),
        out_shape=jax.ShapeDtypeStruct((rows, width), F32),
        in_specs=[pl.BlockSpec(memory_space=pl.ANY)] * 3,
        out_specs=pl.BlockSpec(memory_space=pltpu.VMEM),
        scratch_shapes=[
            pltpu.VMEM((ITERS,) + packed, F32),
            pltpu.VMEM((ITERS, n_blk) + packed, F32),
            pltpu.VMEM((ITERS, n_mem) + packed, F32),
            pltpu.VMEM((band_len, slab), F32),
            pltpu.VMEM((band_len, slab), F32),
            pltpu.VMEM((band_len, slab), jnp.int32),
            pltpu.VMEM((band_len, slab), jnp.int32),
            pltpu.VMEM((ITERS, n_mem) + packed, F32),
            pltpu.VMEM((ITERS, n_mem) + packed, F32),
            pltpu.VMEM((n_mem,) + packed, F32),
            pltpu.VMEM((n_mem,) + packed, F32),
            dma((3,)),
            dma((ITERS, n_blk)), dma((ITERS, n_blk)),
            dma((ITERS, n_mem)), dma((ITERS, n_mem)),
            dma((ITERS, n_mem)), dma((ITERS, n_mem)),
            dma((n_mem,)), dma((n_mem,)),
        ],
        compiler_params=pltpu.CompilerParams(collective_id=0, has_side_effects=True),
        name="majorize",
    )(coords, codes.reshape(band_len, slab), classes.reshape(band_len, slab))


def solution(mesh):
    n_blk, n_mem = mesh.shape["blk"], mesh.shape["member"]
    in_specs = (P(("blk", "member"), None), P("blk", "member", None), P("blk", "member", None))
    out_specs = P(("blk", "member"), None)
    return jax.shard_map(functools.partial(body, n_blk, n_mem), mesh=mesh, in_specs=in_specs, out_specs=out_specs, check_vma=False)
```

time: 149 us -> 37.3 us (0.25)
  blocking collectives: 100 us -> 0 us
  Pallas kernels: 0 us -> 33.5 us
  waiting for transfers between devices: 21 us -> 0 us
  between operations: 13.9 us -> 0.01 us
  matrix products: 7.56 us -> 0 us
  other arithmetic: 4.12 us -> 0 us
  local copies, waits for them, and re-layouts: 1.55 us -> 3.63 us
    all_gather x6 -> x0, blocking collectives: 70.3 us -> none  [the longest x3 42.2 us: body(): band = lax.all_gather(own_rows, 'member', axis=0, tiled=True)]
    pallas_call x0 -> x1, Pallas kernels: none -> 33.5 us  [body(): pl.pallas_call(functools.partial(kernel, n_blk, n_mem), out_shape=jax.Sha...]
    unnamed x3 -> x0, blocking collectives: 30.1 us -> none
    reduce_scatter x3 -> x0, waiting for transfers between devices: 21 us -> none  [body(): lax.psum_scatter(numer, 'member', scatter_dimension=0, tiled=True)]
    dot_general x6 -> x0, matrix products: 7.56 us -> none  [the longest x3 3.9 us: body(): numer = jnp.dot(weights - ratio, columns, precision=lax.Precision.HIGHEST)]
    div x4 -> x0, other arithmetic: 3.14 us -> none  [the longest x3 3.13 us: body(): own_rows = (numer + own_rows * ratio_rows[:, None]) / weight_own[:, None]]
    unnamed x13 -> x2, local copies, waits for them, and re-layouts: 1.55 us -> 3.63 us
  transfers between devices with their start and end apart: 3 -> 0, of which waited for: 3 -> 0; matrix products, arithmetic and copies ran while one was open for 1% -> 0% of each run, Pallas kernels for 0% -> 0%
where the time goes in v1:
time: 37.3 us; the launch traced here: 37.1 us
  Pallas kernels  33.5 us (90%)
  local copies, waits for them, and re-layouts  3.63 us (10%)
    pallas_call x1, Pallas kernels, body(): pl.pallas_call(functools.partial(kernel, n_blk, n_mem), out_shape=jax.Sha...  33.5 us
    unnamed x2, local copies, waits for them, and re-layouts  3.63 us

profile of v1, /device:TPU:0, one launch (start us, length us, event | category | flops | bytes accessed | tf_op | source)
XLA Modules:
  0.0 37.1 jit_solution(5101841017773982574)
XLA Ops:
  0.0 2.3 %copy_bitcast_fusion = (s32[256,512]{1,0:T(8,128)}, s32[256,512]{1,0:T(8,128)}) fusion(s32[256,1,512]{2,1,0:T(1,128)} %param.5, s32[256,1,512]{2,1,0:T(1,128)} %param.4), kind=kLoop, calls=%fused_computation | loop fusion | bytes 2097152
  2.3 33.5 %majorize.1 = f32[64,64]{1,0:T(8,128)} custom-call(f32[64,64]{1,0:T(8,128)} %coords.1, s32[256,512]{1,0:T(8,128)} %get-tuple-element.6.codes, s32[256,512]{1,0:T(8,128)} %get-tuple-element.5.classes), custom_call_target="tpu_custom_call" | custom-call | tf_op jit(solution)/shard_map/majorize/pallas_call | solution.py:184
  35.8 1.4 %copy.9 = f32[64,64]{1,0:T(8,128)} copy(f32[64,64]{1,0:T(8,128)} %majorize.1) | data formatting | bytes 32768

commit v2 on v1

--- a/solution.py
+++ b/solution.py
@@ -62,19 +62,35 @@
     return gram, jnp.concatenate([hm, jnp.where(low, l, 0.0).astype(BF16)], axis=1)
 
 
+def near_first(at, n):
+    if n & (n - 1):
+        return [lax.rem(at + k, n) for k in range(1, n)]
+    flips = [(bit, bit * (1 - 2 * lax.rem(at // bit, 2))) for bit in (1 << i for i in range(n.bit_length() - 1))]
+    return [at + sum(flip for bit, flip in flips if k & bit) for k in range(1, n)]
+
+
+def far_first(at, n):
+    low, high, found = 0, n - 1, []
+    for _ in range(n - 1):
+        pick = (2 * at - low - high + n) // n
+        found.append(high + pick * (low - high))
+        low, high = low + pick, high - 1 + pick
+    return found
+
+
 def kernel(n_blk, n_mem, coords, codes, classes, out,
-           own, columns, band, weights, targets, code_tile, class_tile, part, part_in, wsum, wsum_in,
+           own, columns, band, weights, targets, code_tile, class_tile, gram_side, sum_side, part, part_in, wsum, wsum_in,
            load_sem, col_send, col_recv, band_send, band_recv, part_send, part_recv, w_send, w_recv):
     blk, mem = lax.axis_index("blk"), lax.axis_index("member")
     rows, width = coords.shape
     half = rows // 2
-    slab = codes.shape[1]
-    blks = [lax.rem(blk + k, n_blk) for k in range(1, n_blk)]
-    mems = [lax.rem(mem + k, n_mem) for k in range(1, n_mem)]
+    slab = codes.shape[2]
+    blks = near_first(blk, n_blk)
+    mems = far_first(mem, n_mem)
 
     loads = [pltpu.make_async_copy(coords, out, load_sem.at[0]),
-             pltpu.make_async_copy(codes, code_tile, load_sem.at[1]),
-             pltpu.make_async_copy(classes, class_tile, load_sem.at[2])]
+             pltpu.make_async_copy(classes.at[:, 0, :], class_tile, load_sem.at[1]),
+             pltpu.make_async_copy(codes.at[:, 0, :], code_tile, load_sem.at[2])]
     for load in loads:
         load.start()
     barrier = pltpu.get_barrier_semaphore()
@@ -101,10 +117,10 @@
 
     def spread(it, packed):
         own[it] = packed
-        for b in blks:
-            col_copy(it, b, blk).start()
         for m in mems:
             band_copy(it, m, mem).start()
+        for b in reversed(blks):
+            col_copy(it, b, blk).start()
         columns[it, blk] = packed
         band[it, mem] = packed
 
@@ -131,27 +147,30 @@
         w_copy(m, mem).start()
 
     for it in range(ITERS):
-        for b in blks:
-            col_copy(it, b, b).wait_recv()
-        gram_side, sum_side = column_side(doubled(columns[it]))
-        for m in mems:
-            band_copy(it, m, m).wait_recv()
-        total = None
+        for b in [blk] + blks:
+            if b is not blk:
+                col_copy(it, b, b).wait_recv()
+            block = pl.ds(pl.multiple_of(b * rows, rows), rows)
+            gram_side[block, :], sum_side[block, :] = column_side(doubled(columns[it, pl.ds(b, 1)]))
         for m in order:
+            if m is not mem:
+                band_copy(it, m, m).wait_recv()
             at = pl.ds(pl.multiple_of(m * rows, rows), rows)
             twice = doubled(band[it, pl.ds(m, 1)])
-            dist_sq = lax.dot_general(row_side(twice), gram_side, (((1,), (1,)), ((), ())), preferred_element_type=F32)
+            dist_sq = lax.dot_general(row_side(twice), gram_side[...], (((1,), (1,)), ((), ())), preferred_element_type=F32)
             ratio = targets[at, :] * lax.rsqrt(jnp.maximum(dist_sq, 0.0) + epsilon)
             pull = weights[at, :] - ratio
             high = pull.astype(BF16)
             low = (pull - high.astype(F32)).astype(BF16)
-            sums = jnp.dot(jnp.concatenate([high, low], axis=0), sum_side, preferred_element_type=F32)
+            sums = jnp.dot(jnp.concatenate([high, low], axis=0), sum_side[...], preferred_element_type=F32)
             sums = sums[:rows] + sums[rows:]
             sums = sums[:, : 2 * width] + sums[:, 2 * width:]
             sums = sums + jnp.concatenate([sums[:, width:], sums[:, :width]], axis=1)
-            total = pack(sums + twice * jnp.sum(ratio, axis=1, keepdims=True))
-            if m is not mem:
-                part[it, m] = total
+            packed = pack(sums + twice * jnp.sum(ratio, axis=1, keepdims=True))
+            if m is mem:
+                total = packed
+            else:
+                part[it, m] = packed
                 part_copy(it, m, mem).start()
         if it == 0:
             weight_own = wsum[mem]
@@ -194,6 +213,8 @@
             pltpu.VMEM((band_len, slab), F32),
             pltpu.VMEM((band_len, slab), jnp.int32),
             pltpu.VMEM((band_len, slab), jnp.int32),
+            pltpu.VMEM((slab, 4 * LANES), BF16),
+            pltpu.VMEM((slab, 4 * width), BF16),
             pltpu.VMEM((ITERS, n_mem) + packed, F32),
             pltpu.VMEM((ITERS, n_mem) + packed, F32),
             pltpu.VMEM((n_mem,) + packed, F32),
@@ -206,7 +227,7 @@
         ],
         compiler_params=pltpu.CompilerParams(collective_id=0, has_side_effects=True),
         name="majorize",
-    )(coords, codes.reshape(band_len, slab), classes.reshape(band_len, slab))
+    )(coords, codes, classes)
 
 
 def solution(mesh):

time: 37.3 us -> 34.6 us (0.928)
  local copies, waits for them, and re-layouts: 3.63 us -> 1.38 us
  Pallas kernels: 33.5 us -> 33 us
    unnamed x2 -> x1, local copies, waits for them, and re-layouts: 3.63 us -> 1.38 us
    pallas_call x1, Pallas kernels: 33.5 us -> 33 us  [body(): pl.pallas_call(functools.partial(kernel, n_blk, n_mem), out_shape=jax.Sha...]
where the time goes in v2:
time: 34.6 us; the launch traced here: 34.4 us
  Pallas kernels  33 us (95%)
  local copies, waits for them, and re-layouts  1.38 us (4%)
    pallas_call x1, Pallas kernels, body(): pl.pallas_call(functools.partial(kernel, n_blk, n_mem), out_shape=jax.Sha...  33 us
    unnamed x1, local copies, waits for them, and re-layouts  1.38 us

profile of v2, /device:TPU:0, one launch (start us, length us, event | category | flops | bytes accessed | tf_op | source)
XLA Modules:
  0.0 34.4 jit_solution(2170270361777285722)
XLA Ops:
  0.0 33.0 %majorize.1 = f32[64,64]{1,0:T(8,128)} custom-call(f32[64,64]{1,0:T(8,128)} %coords.1, s32[256,1,512]{2,1,0:T(1,128)} %codes.1, s32[256,1,512]{2,1,0:T(1,128)} %classes.1), custom_call_target="tpu_custom_call" | custom-call | tf_op jit(solution)/shard_map/majorize/pallas_call | solution.py:203
  33.0 1.4 %copy.5 = f32[64,64]{1,0:T(8,128)} copy(f32[64,64]{1,0:T(8,128)} %majorize.1) | data formatting | bytes 32768

commit v3 on v2

--- a/solution.py
+++ b/solution.py
@@ -147,31 +147,39 @@
         w_copy(m, mem).start()
 
     for it in range(ITERS):
-        for b in [blk] + blks:
-            if b is not blk:
-                col_copy(it, b, b).wait_recv()
-            block = pl.ds(pl.multiple_of(b * rows, rows), rows)
-            gram_side[block, :], sum_side[block, :] = column_side(doubled(columns[it, pl.ds(b, 1)]))
-        for m in order:
-            if m is not mem:
-                band_copy(it, m, m).wait_recv()
-            at = pl.ds(pl.multiple_of(m * rows, rows), rows)
-            twice = doubled(band[it, pl.ds(m, 1)])
+        arriving = [blk] + blks
+        for pair in [arriving[k:k + 2] for k in range(0, n_blk, 2)]:
+            for b in pair:
+                if b is not blk:
+                    col_copy(it, b, b).wait_recv()
+            gram, sums = column_side(doubled(jnp.concatenate([columns[it, pl.ds(b, 1)] for b in pair], axis=0)))
+            for k, b in enumerate(pair):
+                block = pl.ds(pl.multiple_of(b * rows, rows), rows)
+                gram_side[block, :], sum_side[block, :] = gram[k * rows:(k + 1) * rows], sums[k * rows:(k + 1) * rows]
+        for m in mems:
+            band_copy(it, m, m).wait_recv()
+        for group in [mems, [mem]]:
+            ats = [pl.ds(pl.multiple_of(m * rows, rows), rows) for m in group]
+            twice = jnp.concatenate([doubled(band[it, pl.ds(m, 1)]) for m in group], axis=0)
             dist_sq = lax.dot_general(row_side(twice), gram_side[...], (((1,), (1,)), ((), ())), preferred_element_type=F32)
-            ratio = targets[at, :] * lax.rsqrt(jnp.maximum(dist_sq, 0.0) + epsilon)
-            pull = weights[at, :] - ratio
+            target = jnp.concatenate([targets[at, :] for at in ats], axis=0)
+            weight = jnp.concatenate([weights[at, :] for at in ats], axis=0)
+            ratio = target * lax.rsqrt(jnp.maximum(dist_sq, 0.0) + epsilon)
+            pull = weight - ratio
             high = pull.astype(BF16)
             low = (pull - high.astype(F32)).astype(BF16)
             sums = jnp.dot(jnp.concatenate([high, low], axis=0), sum_side[...], preferred_element_type=F32)
-            sums = sums[:rows] + sums[rows:]
+            sums = sums[:rows * len(group)] + sums[rows * len(group):]
             sums = sums[:, : 2 * width] + sums[:, 2 * width:]
             sums = sums + jnp.concatenate([sums[:, width:], sums[:, :width]], axis=1)
-            packed = pack(sums + twice * jnp.sum(ratio, axis=1, keepdims=True))
-            if m is mem:
-                total = packed
-            else:
-                part[it, m] = packed
-                part_copy(it, m, mem).start()
+            sums = sums + twice * jnp.sum(ratio, axis=1, keepdims=True)
+            for at, m in enumerate(group):
+                packed = pack(sums[at * rows:(at + 1) * rows])
+                if m is mem:
+                    total = packed
+                else:
+                    part[it, m] = packed
+                    part_copy(it, m, mem).start()
         if it == 0:
             weight_own = wsum[mem]
             for m in mems:
@@ -202,7 +210,7 @@
     dma = pltpu.SemaphoreType.DMA
     return pl.pallas_call(
         functools.partial(kernel, n_blk, n_mem),
-        out_shape=jax.ShapeDtypeStruct((rows, width), F32),
+        out_shape=pltpu.VMEM((rows, width), F32),
         in_specs=[pl.BlockSpec(memory_space=pl.ANY)] * 3,
         out_specs=pl.BlockSpec(memory_space=pltpu.VMEM),
         scratch_shapes=[

time: 34.6 us -> 32 us (0.925)
  Pallas kernels: 33 us -> 31.3 us
  local copies, waits for them, and re-layouts: 1.38 us -> 0.62 us
    pallas_call x1, Pallas kernels: 33 us -> 31.3 us  [body(): pl.pallas_call(functools.partial(kernel, n_blk, n_mem), out_shape=pltpu.V...]
    unnamed x1, local copies, waits for them, and re-layouts: 1.38 us -> 0.62 us
where the time goes in v3:
time: 32 us; the launch traced here: 31.9 us
  Pallas kernels  31.3 us (98%)
  local copies, waits for them, and re-layouts  0.62 us (2%)
    pallas_call x1, Pallas kernels, body(): pl.pallas_call(functools.partial(kernel, n_blk, n_mem), out_shape=pltpu.V...  31.3 us

profile of v3, /device:TPU:0, one launch (start us, length us, event | category | flops | bytes accessed | tf_op | source)
XLA Modules:
  0.0 31.9 jit_solution(4828231814017359501)
XLA Ops:
  0.0 31.3 %majorize.1 = f32[64,64]{1,0:T(8,128)S(1)} custom-call(f32[64,64]{1,0:T(8,128)} %coords.1, s32[256,1,512]{2,1,0:T(1,128)} %codes.1, s32[256,1,512]{2,1,0:T(1,128)} %classes.1), custom_call_target="tpu_custom_call" | custom-call | tf_op jit(solution)/shard_map/majorize/pallas_call | solution.py:211
  31.3 0.6 %copy.5 = f32[64,64]{1,0:T(8,128)} copy(f32[64,64]{1,0:T(8,128)S(1)} %majorize.1) | data formatting | bytes 32768

commit v4 on v3

--- a/solution.py
+++ b/solution.py
@@ -59,7 +59,7 @@
     low, (h, m, l), norm = factors(twice)
     hm = jnp.where(low, h, m).astype(BF16)
     gram = jnp.concatenate([hm, hm, jnp.where(low, l, h).astype(BF16), norm_lanes(norm, twice.shape[0], 0, 3)], axis=1)
-    return gram, jnp.concatenate([hm, jnp.where(low, l, 0.0).astype(BF16)], axis=1)
+    return gram, jnp.concatenate([hm, jnp.where(low, l, 1.0).astype(BF16)], axis=1)
 
 
 def near_first(at, n):
@@ -148,7 +148,7 @@
 
     for it in range(ITERS):
         arriving = [blk] + blks
-        for pair in [arriving[k:k + 2] for k in range(0, n_blk, 2)]:
+        for pair in [arriving[:n_blk // 2], arriving[n_blk // 2:]]:
             for b in pair:
                 if b is not blk:
                     col_copy(it, b, b).wait_recv()
@@ -170,11 +170,14 @@
             low = (pull - high.astype(F32)).astype(BF16)
             sums = jnp.dot(jnp.concatenate([high, low], axis=0), sum_side[...], preferred_element_type=F32)
             sums = sums[:rows * len(group)] + sums[rows * len(group):]
-            sums = sums[:, : 2 * width] + sums[:, 2 * width:]
+            lane = lax.broadcasted_iota(jnp.int32, (rows * len(group), 2 * width), 1)
+            extra = sums[:, 2 * width:]
+            sums = sums[:, : 2 * width] + jnp.where(lane < width, extra, 0.0)
             sums = sums + jnp.concatenate([sums[:, width:], sums[:, :width]], axis=1)
-            sums = sums + twice * jnp.sum(ratio, axis=1, keepdims=True)
+            pulled = jnp.where(lane < width, jnp.concatenate([extra[:, width:], extra[:, :width]], axis=1), extra)
             for at, m in enumerate(group):
-                packed = pack(sums[at * rows:(at + 1) * rows])
+                span = slice(at * rows, (at + 1) * rows)
+                packed = pack(sums[span]) + band[it, m] * (wsum[m] - pack(pulled[span]))
                 if m is mem:
                     total = packed
                 else:
@@ -185,10 +188,11 @@
             for m in mems:
                 w_copy(m, m).wait_recv()
                 weight_own = weight_own + wsum_in[m]
+            inverse = 1.0 / weight_own
         for m in mems:
             part_copy(it, m, m).wait_recv()
             total = total + part_in[it, m]
-        total = total / weight_own
+        total = total * inverse
         if it < ITERS - 1:
             spread(it + 1, total)
     out[...] = jnp.concatenate([total[:, :width], total[:, width:]], axis=0)

time: 32 us -> 31.7 us (level)
  Pallas kernels: 31.3 us -> 30.9 us
where the time goes in v4:
time: 31.7 us; the launch traced here: 31.6 us
  Pallas kernels  30.9 us (97%)
  local copies, waits for them, and re-layouts  0.62 us (2%)
    pallas_call x1, Pallas kernels, body(): pl.pallas_call(functools.partial(kernel, n_blk, n_mem), out_shape=pltpu.V...  30.9 us

profile of v4, /device:TPU:0, one launch (start us, length us, event | category | flops | bytes accessed | tf_op | source)
XLA Modules:
  0.0 31.6 jit_solution(14996364375888059646)
XLA Ops:
  0.0 30.9 %majorize.1 = f32[64,64]{1,0:T(8,128)S(1)} custom-call(f32[64,64]{1,0:T(8,128)} %coords.1, s32[256,1,512]{2,1,0:T(1,128)} %codes.1, s32[256,1,512]{2,1,0:T(1,128)} %classes.1), custom_call_target="tpu_custom_call" | custom-call | tf_op jit(solution)/shard_map/majorize/pallas_call | solution.py:215
  30.9 0.6 %copy.5 = f32[64,64]{1,0:T(8,128)} copy(f32[64,64]{1,0:T(8,128)S(1)} %majorize.1) | data formatting | bytes 32768
